TPU v7x, 512 devices: a whole 4x4x16 slice. The times are simulated.
512 devices in a mesh: dp: 8 (over x, z_hi), row: 8 (over y, core), col: 8 (over z_lo).
Axes of the slice: x: 4, y: 4, z: 16 (z_hi: 2, z_lo: 8; z = z_hi * 8 + z_lo), core: 2. Of those that a mesh axis runs over, the one named last changes fastest.
Arguments:
- inputs: bfloat16 [8, 1024, 4096], P('dp', 'col', 'row'), may hold values from -6 to 6
- weights: bfloat16 [4096, 3, 4096], P('row', None, 'col'), may hold values from -0.09375 to 0.09375
- feature_taps: float32 [3, 3, 4096], P(None, None, 'col'), may hold values from -2.5 to 2.5
- inner_taps: float32 [7, 4096], P(None, 'col'), may hold values from -2.5 to 2.5
- grad_out: bfloat16 [8, 1024, 4096], P('dp', 'row', 'col'), may hold values from -6 to 6
Outputs:
- grad_in: bfloat16 [8, 1024, 4096], P('dp', 'col', 'row')
- grad_weights: float32 [4096, 3, 4096], P('row', None, 'col')
All inputs are finite; a program needn't handle non-finite values.
Results may differ from a plain program's by a relative error of at most 0.033.
Values may be sent and summed in bfloat16 or wider, within the bound.
A program may use at most 64 MiB of HBM per device.

v0:
```python
import jax
import jax.numpy as jnp
from jax import lax
from jax.sharding import PartitionSpec as P


def with_halo(cells, sides, width):
    for axis, dim in sides:
        count = lax.axis_size(axis)
        ends = count - 1
        head = lax.slice_in_dim(cells, 0, width, axis=dim)
        tail = lax.slice_in_dim(cells, cells.shape[dim] - width, cells.shape[dim], axis=dim)
        cells = jnp.concatenate(
            [
                lax.ppermute(tail, axis, [(i, (i + 1) % count) for i in range(ends)]),
                cells,
                lax.ppermute(head, axis, [((i + 1) % count, i) for i in range(ends)]),
            ],
            axis=dim,
        )
    return cells


def shifted(shard, axis, by):
    length = lax.axis_size(axis)
    pairs = [(i, i + by) for i in range(length) if 0 <= i + by < length]
    return lax.ppermute(shard, axis, pairs)


def causal(seq, taps):
    total = taps[0] * seq
    for lag in range(1, taps.shape[0]):
        pad = jnp.zeros((lag,) + seq.shape[1:], jnp.float32)
        total = total + taps[lag] * jnp.concatenate([pad, seq[:-lag]], axis=0)
    return total


def anticausal(seq, taps):
    total = taps[0] * seq
    for lag in range(1, taps.shape[0]):
        pad = jnp.zeros((lag,) + seq.shape[1:], jnp.float32)
        total = total + taps[lag] * jnp.concatenate([seq[lag:], pad], axis=0)
    return total


def rounded(value):
    return lax.optimization_barrier(value.astype(jnp.bfloat16)).astype(jnp.float32)


def on_device(inputs, weights, feature_taps, inner_taps, grad_out):
    tile = inputs[0]
    upstream_tile = grad_out[0]
    rows_dev = upstream_tile.shape[0]
    width_row = weights.shape[0]
    width_col = weights.shape[2]
    margin = feature_taps.shape[0] - 1 + (inner_taps.shape[0] - 1)
    flat_w = weights.reshape(width_row, 3 * width_col)
    columns = lax.all_gather(tile, "col", axis=0, tiled=True)
    block = columns
    proj = lax.psum_scatter(
        jnp.dot(block, flat_w, preferred_element_type=jnp.float32).astype(jnp.bfloat16),
        "row",
        scatter_dimension=0,
        tiled=True,
    )
    padded = with_halo(proj, (("row", 0),), margin)
    after = shifted(upstream_tile[:margin], "row", -1)
    length = rows_dev + 2 * margin
    window = padded.astype(jnp.float32).reshape(length, 3, width_col)
    upstream = jnp.concatenate(
        [
            jnp.zeros((margin, width_col), jnp.float32),
            upstream_tile.astype(jnp.float32),
            after.astype(jnp.float32),
        ],
        axis=0,
    )
    mixed = causal(window, feature_taps)
    query = mixed[:, 0]
    key = mixed[:, 1]
    value = mixed[:, 2]
    product = rounded(key * value)
    inner = causal(product, inner_taps)
    grad_query = upstream * inner
    grad_inner = upstream * query
    grad_product = anticausal(grad_inner, inner_taps)
    grad_mixed = jnp.stack([grad_query, grad_product * value, grad_product * key], axis=1)
    grad_proj = anticausal(grad_mixed, feature_taps)[margin : margin + rows_dev].astype(
        jnp.bfloat16
    )
    gathered = lax.all_gather(grad_proj.reshape(rows_dev, 3 * width_col), "row", axis=0, tiled=True)
    block = gathered
    grad_x = lax.psum_scatter(
        lax.dot_general(
            block, flat_w, (((1,), (1,)), ((), ())), preferred_element_type=jnp.float32
        ).astype(jnp.bfloat16),
        "col",
        scatter_dimension=0,
        tiled=True,
    )
    local = lax.dot_general(
        columns, gathered, (((0,), (0,)), ((), ())), preferred_element_type=jnp.float32
    )
    grad_w = lax.psum(local.astype(jnp.bfloat16), "dp").astype(jnp.float32)
    return (grad_x[None], grad_w.reshape(width_row, 3, width_col))


def solution(mesh):
    placed = (
        P("dp", "col", "row"),
        P("row", None, "col"),
        P(None, None, "col"),
        P(None, "col"),
        P("dp", "row", "col"),
    )
    return jax.shard_map(
        on_device,
        mesh=mesh,
        in_specs=placed,
        out_specs=(P("dp", "col", "row"), P("row", None, "col")),
        check_vma=False,
    )
```

profile of v0, /device:TPU:4, one launch (start us, length us, event | category | flops | bytes accessed | tf_op | source)
XLA Modules:
  0.0 570.4 jit_solution(13624536837322378949)
XLA Ops:
  7.2 0.7 all-gather.6.cloned.1.call-update
  7.9 1.7 copy.13
  9.7 72.3 %all-gather.6.cloned.1.call-done = bf16[1,1024,512]{2,1,0:T(8,128)(2,1)} async-done(((bf16[1,128,512]{2,1,0:T(8,128)(2,1)}), bf16[1,1024,512]{2,1,0:T(8,128)(2,1)}) %all-gather.6.cloned.1.call-update) | async-done | bytes 1048592 | tf_op jit(solution)/shard_map/all_gather | solution.py:58
  82.0 4.7 convolution_convert_fusion
  86.8 0.8 copy-done.3
  87.7 1.3 collective-permute-start
  89.1 34.9 %reduce-scatter.3.cloned.1.call-done = bf16[128,1536]{1,0:T(8,128)(2,1)} async-done(((bf16[1024,1536]{1,0:T(8,128)(2,1)}), bf16[128,1536]{1,0:T(8,128)(2,1)}) %reduce-scatter.3.cloned.1.call-update) | async-done | bytes 393232 | tf_op jit(solution)/shard_map/reduce_scatter | solution.py:60
  124.0 0.8 fusion.6
  124.8 1.3 collective-permute-start.2
  126.1 3.0 collective-permute-start.1
  129.2 1.2 copy.14
  131.1 1.6 copy.20
  133.1 3.2 multiply_add_fusion
  137.8 0.8 multiply_bitcast_fusion.1
  139.0 1.8 multiply_bitcast_fusion.2
  141.8 2.1 fusion.3
  144.0 39.6 %all-gather.4.cloned.1.call-done = bf16[1024,1536]{0,1:T(8,128)(2,1)} async-done(((bf16[128,1536]{0,1:T(8,128)(2,1)}), bf16[1024,1536]{0,1:T(8,128)(2,1)}) %all-gather.4.cloned.1.call-update) | async-done | bytes 3145744 | tf_op jit(solution)/shard_map/all_gather | solution.py:91
  183.5 3.7 convolution_convert_fusion.1
  187.2 1.6 copy.19
  188.9 1.3 copy-done.2
  190.2 4.7 convolution_convert_fusion.2
  194.9 294.7 %all-reduce.18.cloned.1.call-done = bf16[512,3,512]{2,0,1:T(8,128)(2,1)} async-done(((bf16[512,3,512]{2,0,1:T(8,128)(2,1)}), bf16[512,3,512]{2,0,1:T(8,128)(2,1)}) %all-reduce.18.cloned.1.call-update) | async-done | bytes 1572880 | tf_op jit(solution)/shard_map/psum | solution.py:104
  489.6 3.5 reshape.28
  493.1 70.8 %reduce-scatter.5.cloned.1.call-done = bf16[128,512]{1,0:T(8,128)(2,1)} async-done(((bf16[1024,512]{1,0:T(8,128)(2,1)}), bf16[128,512]{1,0:T(8,128)(2,1)}) %reduce-scatter.5.cloned.1.call-update) | async-done | bytes 131088 | tf_op jit(solution)/shard_map/reduce_scatter | solution.py:93
  (53 shorter events, 4.3 us)
Async XLA Ops:
  7.2 74.8 %all-gather.6.cloned.1.call-start = ((), (), s32[]{:S(2)}) async-start(), calls=%async_computation.6 | async-start | bytes 1179648 | tf_op jit(solution)/shard_map/all_gather | solution.py:58
  7.9 116.1 %reduce-scatter.3.cloned.1.call-start = ((), (), s32[]{:S(2)}) async-start(), calls=%async_computation.2 | async-start | bytes 3538944 | tf_op jit(solution)/shard_map/reduce_scatter | solution.py:60
  9.7 77.0 %copy-start.1 = (bf16[512,3,512]{0,2,1:T(8,128)(2,1)}, bf16[512,3,512]{0,2,1:T(8,128)(2,1)S(1)}, u32[]{:S(2)}) copy-start(bf16[512,3,512]{0,2,1:T(8,128)(2,1)S(1)} %copy.13) | copy-start | bytes 4718596
  86.7 0.9 copy-start.3
  86.7 2.3 copy-start.4
  86.7 42.5 %copy-start.5 = (f32[7,512]{1,0:T(8,128)S(1)}, f32[7,512]{1,0:T(8,128)}, u32[]{:S(2)}) copy-start(f32[7,512]{1,0:T(8,128)} %param.8) | copy-start | bytes 43012
  86.7 96.8 %all-gather.4.cloned.1.call-start = ((), (), s32[]{:S(2)}) async-start(), calls=%async_computation.3 | async-start | bytes 3538944 | tf_op jit(solution)/shard_map/all_gather | solution.py:91
  87.7 41.5 %collective-permute-start = (bf16[8,512]{0,1:T(8,128)(2,1)S(1)}, bf16[8,512]{0,1:T(8,128)(2,1)S(1)}, u32[]{:S(2)}, u32[]{:S(2)}) collective-permute-start(bf16[8,512]{0,1:T(8,128)(2,1)S(1)} %slice_bitcast_fusion.3), channel_id=1, source_target_pairs={{8,0},{16,8},{24,16},{32,24},{40,32},{48,40},{56,48},{9,1},{17,9},... | collective-permute-start | bytes 24584 | tf_op jit(solution)/shard_map/ppermute | solution.py:27
  124.0 6.5 %copy-start = (bf16[128,1536]{1,0:T(8,128)(2,1)S(1)}, bf16[128,1536]{1,0:T(8,128)(2,1)}, u32[]{:S(2)}) copy-start(bf16[128,1536]{1,0:T(8,128)(2,1)} %reduce-scatter.3.cloned.1.call-done) | copy-start | bytes 1179652
  124.8 5.6 collective-permute-start.2
  126.1 4.4 collective-permute-start.1
  141.8 41.7 %copy-start.6 = (bf16[1,1024,512]{2,1,0:T(8,128)(2,1)S(1)}, bf16[1,1024,512]{2,1,0:T(8,128)(2,1)}, u32[]{:S(2)}) copy-start(bf16[1,1024,512]{2,1,0:T(8,128)(2,1)} %all-gather.6.cloned.1.call-done) | copy-start | bytes 3145732
  143.9 345.7 %all-reduce.18.cloned.1.call-start = ((), (), s32[]{:S(2)}) async-start(), calls=%async_computation.5 | async-start | bytes 3145728 | tf_op jit(solution)/shard_map/psum | solution.py:104
  188.8 1.4 copy-start.2
  188.8 375.0 %reduce-scatter.5.cloned.1.call-start = ((), (), s32[]{:S(2)}) async-start(), calls=%async_computation.4 | async-start | bytes 1179648 | tf_op jit(solution)/shard_map/reduce_scatter | solution.py:93
Sparse Core Ops, SparseCore 0:
  10.1 71.8 all-gather.5
  86.8 37.1 reduce-scatter.2
  144.0 39.4 all-gather.3
  188.9 300.5 all-reduce.17
  492.8 70.9 reduce-scatter.4
where the time goes:
time: 571 us; the launch traced here: 570 us
  waiting for transfers between devices  513 us (90%)
  between operations  14.1 us (2%)
  matrix products  13.1 us (2%)
  local copies, waits for them, and re-layouts  12.5 us (2%)
  other arithmetic  11.9 us (2%)
  starting transfers between devices  5.8 us (1%)
    psum x1, waiting for transfers between devices, on_device(): grad_w = lax.psum(local.astype(jnp.bfloat16), 'dp').astype(jnp.float32)  295 us
    all_gather x1, waiting for transfers between devices, on_device(): columns = lax.all_gather(tile, 'col', axis=0, tiled=True)  72.3 us
    reduce_scatter x1, waiting for transfers between devices, on_device(): lax.psum_scatter(lax.dot_general(block, flat_w, (((1,), (1,)), ((), ())),...  70.8 us
    all_gather x1, waiting for transfers between devices, on_device(): lax.all_gather(grad_proj.reshape(rows_dev, 3 * width_col), 'row', axis=0,...  39.6 us
    reduce_scatter x1, waiting for transfers between devices, on_device(): lax.psum_scatter(jnp.dot(block, flat_w, preferred_element_type=jnp.float3...  34.9 us
  transfers between devices with their start and end apart: 8, of which 5 were waited for; matrix products, arithmetic and copies ran while one was open for 2% of the time, Pallas kernels for 0%

commit v1 on v0

--- a/solution.py
+++ b/solution.py
@@ -101,7 +101,7 @@
     local = lax.dot_general(
         columns, gathered, (((0,), (0,)), ((), ())), preferred_element_type=jnp.float32
     )
-    grad_w = lax.psum(local.astype(jnp.bfloat16), "dp").astype(jnp.float32)
+    grad_w = jnp.sum(lax.all_gather(local.astype(jnp.bfloat16), "dp"), axis=0).astype(jnp.float32)
     return (grad_x[None], grad_w.reshape(width_row, 3, width_col))
 
 

time: 571 us -> 700 us (1.23)
  the two profiles are of different devices: /device:TPU:4 before, /device:TPU:6 now
where the time goes in v1:
time: 700 us; the launch traced here: 699 us
  waiting for transfers between devices  625 us (89%)
  local copies, waits for them, and re-layouts  22.2 us (3%)
  other arithmetic  17.8 us (3%)
  matrix products  14.2 us (2%)
  between operations  14.1 us (2%)
    all_gather x1, waiting for transfers between devices, on_device(): lax.all_gather(local.astype(jnp.bfloat16), 'dp')  416 us
    all_gather x1, waiting for transfers between devices, on_device(): columns = lax.all_gather(tile, 'col', axis=0, tiled=True)  72.3 us
    reduce_scatter x1, waiting for transfers between devices, on_device(): lax.psum_scatter(lax.dot_general(block, flat_w, (((1,), (1,)), ((), ())),...  61.7 us
    all_gather x1, waiting for transfers between devices, on_device(): lax.all_gather(grad_proj.reshape(rows_dev, 3 * width_col), 'row', axis=0,...  39.6 us
    reduce_scatter x1, waiting for transfers between devices, on_device(): lax.psum_scatter(jnp.dot(block, flat_w, preferred_element_type=jnp.float3...  34.9 us
    unnamed x18, local copies, waits for them, and re-layouts  15.3 us
  transfers between devices with their start and end apart: 8, of which 5 were waited for; matrix products, arithmetic and copies ran while one was open for 4% of the time, Pallas kernels for 0%

profile of v1, /device:TPU:6, one launch (start us, length us, event | category | flops | bytes accessed | tf_op | source)
XLA Modules:
  0.0 699.2 jit_solution(11496303833266075919)
XLA Ops:
  7.9 1.7 copy.12
  9.7 72.3 %all-gather.8.cloned.1.call-done = bf16[1,1024,512]{2,1,0:T(8,128)(2,1)} async-done(((bf16[1,128,512]{2,1,0:T(8,128)(2,1)}), bf16[1,1024,512]{2,1,0:T(8,128)(2,1)}) %all-gather.8.cloned.1.call-update) | async-done | bytes 1048592 | tf_op jit(solution)/shard_map/all_gather | solution.py:58
  81.9 4.7 convolution_convert_fusion
  86.8 0.8 copy-done.3
  87.7 1.3 collective-permute-start
  89.1 34.9 %reduce-scatter.3.cloned.1.call-done = bf16[128,1536]{1,0:T(8,128)(2,1)} async-done(((bf16[1024,1536]{1,0:T(8,128)(2,1)}), bf16[128,1536]{1,0:T(8,128)(2,1)}) %reduce-scatter.3.cloned.1.call-update) | async-done | bytes 393232 | tf_op jit(solution)/shard_map/reduce_scatter | solution.py:60
  124.0 0.8 fusion.7
  124.8 1.3 collective-permute-start.2
  126.1 3.0 collective-permute-start.1
  129.2 1.2 copy.13
  131.0 1.6 copy.19
  133.1 3.2 multiply_add_fusion
  137.8 0.8 multiply_bitcast_fusion.1
  139.0 1.8 multiply_bitcast_fusion.2
  141.8 2.1 fusion.4
  144.0 39.6 %all-gather.6.cloned.1.call-done = bf16[1024,1536]{0,1:T(8,128)(2,1)} async-done(((bf16[128,1536]{0,1:T(8,128)(2,1)}), bf16[1024,1536]{0,1:T(8,128)(2,1)}) %all-gather.6.cloned.1.call-update) | async-done | bytes 3145744 | tf_op jit(solution)/shard_map/all_gather | solution.py:91
  183.5 4.8 fusion
  188.6 1.2 copy-done.2
  189.8 4.7 convolution_convert_fusion.2
  194.5 415.6 %all-gather.10.cloned.1.call-done = bf16[4096,1536]{0,1:T(8,128)(2,1)} async-done(((bf16[512,1536]{0,1:T(8,128)(2,1)}), bf16[4096,1536]{0,1:T(8,128)(2,1)}) %all-gather.10.cloned.1.call-update) | async-done | bytes 12582928 | tf_op jit(solution)/shard_map/all_gather | solution.py:104
  610.1 9.4 %copy.21 = bf16[192,8,8,512]{3,2,1,0:T(8,128)(2,1)S(1)} copy(bf16[192,8,8,512]{3,1,2,0:T(8,128)(2,1)} %bitcast.68) | data formatting | bytes 25165824
  619.5 9.4 %bitcast_reduce_fusion = bf16[512,1536]{0,1:T(8,128)(2,1)S(1)} fusion(bf16[192,8,8,512]{3,2,1,0:T(8,128)(2,1)S(1)} %copy.21), kind=kLoop, calls=%fused_computation | loop fusion | flops 5505024 | bytes 14155776 | tf_op jit(solution)/shard_map/reduce_sum | solution.py:104
  628.9 2.1 copy.18
  631.0 61.7 %reduce-scatter.5.cloned.1.call-done = bf16[128,512]{1,0:T(8,128)(2,1)} async-done(((bf16[1024,512]{1,0:T(8,128)(2,1)}), bf16[128,512]{1,0:T(8,128)(2,1)}) %reduce-scatter.5.cloned.1.call-update) | async-done | bytes 131088 | tf_op jit(solution)/shard_map/reduce_scatter | solution.py:93
  (54 shorter events, 5.2 us)
Async XLA Ops:
  7.2 74.8 %all-gather.8.cloned.1.call-start = ((), (), s32[]{:S(2)}) async-start(), calls=%async_computation.5 | async-start | bytes 1179648 | tf_op jit(solution)/shard_map/all_gather | solution.py:58
  7.9 116.1 %reduce-scatter.3.cloned.1.call-start = ((), (), s32[]{:S(2)}) async-start(), calls=%async_computation.2 | async-start | bytes 3538944 | tf_op jit(solution)/shard_map/reduce_scatter | solution.py:60
  9.7 77.0 %copy-start.1 = (bf16[512,3,512]{0,2,1:T(8,128)(2,1)}, bf16[512,3,512]{0,2,1:T(8,128)(2,1)S(1)}, u32[]{:S(2)}) copy-start(bf16[512,3,512]{0,2,1:T(8,128)(2,1)S(1)} %copy.12) | copy-start | bytes 4718596
  86.7 0.9 copy-start.3
  86.7 2.3 copy-start.4
  86.7 42.5 %copy-start.5 = (f32[7,512]{1,0:T(8,128)S(1)}, f32[7,512]{1,0:T(8,128)}, u32[]{:S(2)}) copy-start(f32[7,512]{1,0:T(8,128)} %param.8) | copy-start | bytes 43012
  86.7 96.8 %all-gather.6.cloned.1.call-start = ((), (), s32[]{:S(2)}) async-start(), calls=%async_computation.3 | async-start | bytes 3538944 | tf_op jit(solution)/shard_map/all_gather | solution.py:91
  87.7 41.5 %collective-permute-start = (bf16[8,512]{0,1:T(8,128)(2,1)S(1)}, bf16[8,512]{0,1:T(8,128)(2,1)S(1)}, u32[]{:S(2)}, u32[]{:S(2)}) collective-permute-start(bf16[8,512]{0,1:T(8,128)(2,1)S(1)} %slice_bitcast_fusion.3), channel_id=1, source_target_pairs={{8,0},{16,8},{24,16},{32,24},{40,32},{48,40},{56,48},{9,1},{17,9},... | collective-permute-start | bytes 24584 | tf_op jit(solution)/shard_map/ppermute | solution.py:27
  124.0 6.5 copy-start
  124.8 5.6 collective-permute-start.2
  126.1 4.4 collective-permute-start.1
  141.8 41.7 %copy-start.6 = (bf16[1,1024,512]{2,1,0:T(8,128)(2,1)S(1)}, bf16[1,1024,512]{2,1,0:T(8,128)(2,1)}, u32[]{:S(2)}) copy-start(bf16[1,1024,512]{2,1,0:T(8,128)(2,1)} %all-gather.8.cloned.1.call-done) | copy-start | bytes 3145732
  143.9 466.2 %all-gather.10.cloned.1.call-start = ((), (), s32[]{:S(2)}) async-start(), calls=%async_computation.6 | async-start | bytes 14155776 | tf_op jit(solution)/shard_map/all_gather | solution.py:104
  188.4 1.4 copy-start.2
  188.4 504.3 %reduce-scatter.5.cloned.1.call-start = ((), (), s32[]{:S(2)}) async-start(), calls=%async_computation.4 | async-start | bytes 1179648 | tf_op jit(solution)/shard_map/reduce_scatter | solution.py:93
Sparse Core Ops, SparseCore 0:
  10.1 71.8 all-gather.7
  86.8 37.1 reduce-scatter.2
  144.0 39.4 all-gather.5
  188.5 421.5 all-gather.9
  613.3 79.3 reduce-scatter.4
